TPU v7x, 256 devices: a whole 4x4x8 slice. The times are simulated.
256 devices in a mesh: seq: 32 (over z, y), tp: 8 (over x, core).
Axes of the slice: x: 4, y: 4, z: 8, core: 2. Of those that a mesh axis runs over, the one named last changes fastest.
Arguments:
- query_raw: bfloat16 [16384, 4096], P('seq', 'tp'), may hold values from -6 to 6
- key_raw: bfloat16 [16384, 4096], P('seq', 'tp'), may hold values from -6 to 6
- value_raw: bfloat16 [16384, 4096], P('seq', 'tp'), may hold values from -6 to 6
- conv_taps: float32 [3, 4, 4096], P(None, None, 'tp'), may hold values from -3 to 3
- layout_boxes: int32 [4, 16384], P(None, 'seq'), may hold values from 0 to 1023
- box_tables: bfloat16 [2, 1024, 4096], P(None, None, 'tp'), may hold values from -4 to 4
- log_decay: float32 [32, 16384], P('tp', 'seq'), may hold values from -1 to 0, as said below
- norm_gain: float32 [4096], P('tp'), may hold values from 0.25 to 1.75
- out_weight: bfloat16 [4096, 4096], P('tp', 'seq'), may hold values from -0.09375 to 0.09375
- grad_output: bfloat16 [16384, 4096], P('seq', 'tp'), may hold values from -6 to 6
Outputs:
- layer_out: bfloat16 [16384, 4096], P('seq', 'tp')
- grad_query: bfloat16 [16384, 4096], P('seq', 'tp')
- grad_key: bfloat16 [16384, 4096], P('seq', 'tp')
- grad_value: bfloat16 [16384, 4096], P('seq', 'tp')
- grad_taps: float32 [3, 4, 4096], P(None, None, 'tp')
- grad_tables: float32 [2, 1024, 4096], P(None, None, 'tp')
- grad_gain: float32 [4096], P('tp')
- grad_weight: float32 [4096, 4096], P('tp', 'seq')
Inputs may be any that keep to these rules, and one draw needn't show every extreme that they name: `log_decay`: each entry is the logarithm (at most 0) of one head's state decay at one token.
All inputs are finite; a program needn't handle non-finite values.
Results may differ from a plain program's by a relative error of at most 0.02.
Values may be sent and summed in bfloat16 or wider, within the bound.
A program may use at most 128 MiB of HBM per device.

v0:
```python
import jax
import jax.numpy as jnp
from jax import lax
from jax.sharding import PartitionSpec as P

HIGHEST = lax.Precision.HIGHEST


def shifted(x, axis, by):
    length = lax.axis_size(axis)
    pairs = [(i, i + by) for i in range(length) if 0 <= i + by < length]
    return lax.ppermute(x, axis, pairs)


def entering(log_total, state, axis, reverse):
    length = lax.axis_size(axis)
    step = -1 if reverse else 1
    heads, rows, cols = state.shape
    total_rows = jnp.broadcast_to(log_total[:, None, None], (heads, 8, cols))
    packed = shifted(jnp.concatenate([state, total_rows], axis=1), axis, step)
    distance = 1
    while distance < length:
        far = shifted(packed, axis, step * distance)
        near_total = packed[:, rows : rows + 1, :]
        packed = jnp.concatenate(
            [
                jnp.exp(near_total) * far[:, :rows, :] + packed[:, :rows, :],
                far[:, rows:, :] + packed[:, rows:, :],
            ],
            axis=1,
        )
        distance *= 2
    return packed[:, :rows, :]


def on_device(
    query_raw,
    key_raw,
    value_raw,
    conv_taps,
    layout_boxes,
    box_tables,
    log_decay,
    norm_gain,
    out_weight,
    grad_output,
):
    row_count, feat_width = query_raw.shape
    head_count = log_decay.shape[0]
    head_size = feat_width // head_count
    kernel = conv_taps.shape[1]
    buckets = box_tables.shape[1]
    feature_scale = head_size ** (-0.5)
    stacked = jnp.stack([query_raw, key_raw, value_raw])
    rim_rows = shifted(stacked[:, row_count - (kernel - 1) :, :], "seq", 1)
    padded = jnp.concatenate([rim_rows, stacked], axis=1).astype(jnp.float32)
    conved = jnp.zeros((3, row_count, feat_width), jnp.float32)
    for tap_step in range(kernel):
        conved = (
            conved
            + conv_taps[:, tap_step, None, :]
            * padded[:, kernel - 1 - tap_step : kernel - 1 - tap_step + row_count, :]
        )
    bucket_ids = jnp.arange(buckets, dtype=jnp.int32)

    def count_table(first, second):
        return (first[:, None] == bucket_ids[None, :]).astype(jnp.bfloat16) + (
            second[:, None] == bucket_ids[None, :]
        ).astype(jnp.bfloat16)

    hot_x = count_table(layout_boxes[0], layout_boxes[2])
    hot_y = count_table(layout_boxes[1], layout_boxes[3])
    layout = jnp.dot(hot_x, box_tables[0], preferred_element_type=jnp.float32) + jnp.dot(
        hot_y, box_tables[1], preferred_element_type=jnp.float32
    )
    query_feat = (feature_scale * (conved[0] + layout)).astype(jnp.bfloat16)
    key_feat = (conved[1] + layout).astype(jnp.bfloat16)
    value_feat = conved[2].astype(jnp.bfloat16)

    def split_heads(matrix):
        return matrix.reshape(row_count, head_count, head_size).transpose(1, 0, 2)

    def join_heads(blocks):
        return blocks.transpose(1, 0, 2).reshape(row_count, feat_width)

    query_heads = split_heads(query_feat)
    key_heads = split_heads(key_feat)
    value_heads = split_heads(value_feat)
    decay_sum = jnp.cumsum(log_decay, axis=1)
    decay_total = decay_sum[:, -1]
    head_decay = jnp.exp(decay_sum)[:, :, None]
    tail_decay = jnp.exp(decay_total[:, None] - decay_sum)[:, :, None]
    positions = jnp.arange(row_count, dtype=jnp.int32)
    causal_mask = positions[:, None] >= positions[None, :]
    decay_mask = jnp.where(
        causal_mask[None],
        jnp.exp(jnp.minimum(decay_sum[:, :, None] - decay_sum[:, None, :], 0.0)),
        0.0,
    )
    local_state = jnp.einsum("hsi,hsj->hij", key_heads * tail_decay, value_heads, precision=HIGHEST)
    incoming = entering(decay_total, local_state, "seq", False)
    scores = decay_mask * jnp.einsum(
        "hti,hsi->hts", query_heads, key_heads, preferred_element_type=jnp.float32
    )
    attended = jnp.einsum("hts,hsj->htj", scores, value_heads, precision=HIGHEST)
    attended = attended + head_decay * jnp.einsum(
        "hti,hij->htj", query_heads, incoming, precision=HIGHEST
    )
    inverse = lax.rsqrt(jnp.mean(attended * attended, axis=-1, keepdims=True) + 1e-06)
    unit_norm = attended * inverse
    gain_heads = norm_gain.reshape(head_count, 1, head_size)
    normed = join_heads(unit_norm * gain_heads).astype(jnp.bfloat16)
    partial_sum = jnp.dot(
        normed,
        lax.all_gather(out_weight, "seq", axis=1, tiled=True),
        preferred_element_type=jnp.float32,
    )
    layer_out = lax.psum_scatter(
        partial_sum.astype(jnp.bfloat16), "tp", scatter_dimension=1, tiled=True
    )
    cotangent = lax.all_gather(grad_output, "tp", axis=1, tiled=True)
    contract_last = (((1,), (1,)), ((), ()))
    grad_normed_sum = lax.dot_general(
        cotangent,
        lax.all_gather(out_weight, "seq", axis=1, tiled=True),
        contract_last,
        preferred_element_type=jnp.float32,
    )
    grad_normed = grad_normed_sum.astype(jnp.bfloat16)
    contract_first = (((0,), (0,)), ((), ()))
    weight_terms = lax.dot_general(
        normed, cotangent, contract_first, preferred_element_type=jnp.float32
    )
    grad_heads = split_heads(grad_normed).astype(jnp.float32)
    gain_terms = jnp.sum(grad_heads * unit_norm, axis=1).reshape(feat_width)
    grad_unit = grad_heads * gain_heads
    grad_attended = inverse * (
        grad_unit - unit_norm * jnp.mean(grad_unit * unit_norm, axis=-1, keepdims=True)
    )
    back_state = jnp.einsum(
        "hti,htj->hij", query_heads * head_decay, grad_attended, precision=HIGHEST
    )
    later_state = entering(decay_total, back_state, "seq", True)
    seq_count = lax.axis_size("seq")
    col_block = weight_terms.shape[1] // seq_count
    weight_parts = (
        weight_terms.astype(jnp.bfloat16)
        .reshape(feat_width, seq_count, col_block)
        .transpose(1, 0, 2)
    )
    weight_parts, later_state = lax.optimization_barrier((weight_parts, later_state))
    grad_scores = decay_mask * jnp.einsum(
        "htj,hsj->hts", grad_attended, value_heads, precision=HIGHEST
    )
    grad_qh = jnp.einsum(
        "hts,hsi->hti", grad_scores, key_heads, precision=HIGHEST
    ) + head_decay * jnp.einsum("htj,hij->hti", grad_attended, incoming, precision=HIGHEST)
    grad_kh = jnp.einsum(
        "hts,hti->hsi", grad_scores, query_heads, precision=HIGHEST
    ) + tail_decay * jnp.einsum("hsj,hij->hsi", value_heads, later_state, precision=HIGHEST)
    grad_vh = jnp.einsum(
        "hts,htj->hsj", scores, grad_attended, precision=HIGHEST
    ) + tail_decay * jnp.einsum("hsi,hij->hsj", key_heads, later_state, precision=HIGHEST)
    grad_pre = jnp.stack(
        [feature_scale * join_heads(grad_qh), join_heads(grad_kh), join_heads(grad_vh)]
    )
    next_rows = shifted(grad_pre[:, : kernel - 1, :], "seq", -1)
    extended = jnp.concatenate([grad_pre, next_rows], axis=1)
    grad_inputs = jnp.zeros((3, row_count, feat_width), jnp.float32)
    for tap_step in range(kernel):
        grad_inputs = (
            grad_inputs
            + conv_taps[:, tap_step, None, :] * extended[:, tap_step : tap_step + row_count, :]
        )
    tap_terms = jnp.stack(
        [
            jnp.sum(
                grad_pre * padded[:, kernel - 1 - tap_step : kernel - 1 - tap_step + row_count, :],
                axis=1,
            )
            for tap_step in range(kernel)
        ],
        axis=1,
    )
    grad_layout = (grad_pre[0] + grad_pre[1]).astype(jnp.bfloat16)
    table_terms = jnp.stack(
        [
            lax.dot_general(hot_x, grad_layout, contract_first, preferred_element_type=jnp.float32),
            lax.dot_general(hot_y, grad_layout, contract_first, preferred_element_type=jnp.float32),
        ]
    )
    table_rows = 2 * buckets
    tap_rows = 3 * kernel
    packed = jnp.concatenate(
        [
            table_terms.astype(jnp.bfloat16).reshape(table_rows, feat_width),
            tap_terms.astype(jnp.bfloat16).reshape(tap_rows, feat_width),
            gain_terms.astype(jnp.bfloat16).reshape(1, feat_width),
        ]
    )
    packed, layer_out, weight_parts = lax.optimization_barrier((packed, layer_out, weight_parts))
    summed = lax.psum(packed, "seq").astype(jnp.float32)
    weight_parts = lax.all_to_all(weight_parts, "seq", 0, 0, tiled=True)
    grad_weight = jnp.sum(weight_parts.astype(jnp.float32), axis=0)
    grad_tables = summed[:table_rows].reshape(2, buckets, feat_width)
    grad_taps = summed[table_rows : table_rows + tap_rows].reshape(3, kernel, feat_width)
    grad_gain = summed[table_rows + tap_rows]
    grad_query = grad_inputs[0].astype(jnp.bfloat16)
    grad_key = grad_inputs[1].astype(jnp.bfloat16)
    grad_value = grad_inputs[2].astype(jnp.bfloat16)
    return (
        layer_out,
        grad_query,
        grad_key,
        grad_value,
        grad_taps,
        grad_tables,
        grad_gain,
        grad_weight,
    )


def solution(mesh):
    return jax.shard_map(
        on_device,
        mesh=mesh,
        in_specs=(
            P("seq", "tp"),
            P("seq", "tp"),
            P("seq", "tp"),
            P(None, None, "tp"),
            P(None, "seq"),
            P(None, None, "tp"),
            P("tp", "seq"),
            P("tp"),
            P("tp", "seq"),
            P("seq", "tp"),
        ),
        out_specs=(
            P("seq", "tp"),
            P("seq", "tp"),
            P("seq", "tp"),
            P("seq", "tp"),
            P(None, None, "tp"),
            P(None, None, "tp"),
            P("tp"),
            P("tp", "seq"),
        ),
        check_vma=False,
    )
```

profile of v0, /device:TPU:2, one launch (start us, length us, event | category | flops | bytes accessed | tf_op | source)
XLA Modules:
  0.0 490.2 jit_solution(6953520611271623817)
XLA Ops:
  8.0 1.3 copy.79
  9.2 1.3 copy.80
  10.5 1.3 copy.81
  11.9 3.5 collective-permute-start
  15.6 1.2 reduce-window.6
  17.5 2.3 fusion.58
  19.8 4.0 collective-permute-done
  24.6 3.7 multiply_add_fusion
  28.5 1.1 fusion.64
  30.4 1.3 fusion.81
  31.8 4.4 collective-permute-start.1
  36.2 5.0 %collective-permute-done.1 = f32[4,136,128]{2,1,0:T(8,128)S(1)} collective-permute-done((f32[4,136,128]{2,1,0:T(8,128)S(1)}, f32[4,136,128]{2,1,0:T(8,128)S(1)}, u32[]{:S(2)}, u32[]{:S(2)}) %collective-permute-start.1) | collective-permute-done | bytes 278560 | tf_op jit(solution)/shard_map/ppermute | solution.py:12
  41.3 4.4 collective-permute-start.2
  45.7 4.3 collective-permute-done.2
  50.0 6.0 %collective-permute-start.3 = (f32[4,136,128]{2,1,0:T(8,128)S(1)}, f32[4,136,128]{2,1,0:T(8,128)S(1)}, u32[]{:S(2)}, u32[]{:S(2)}) collective-permute-start(f32[4,136,128]{2,1,0:T(8,128)S(1)} %pad_maximum_fusion.7), channel_id=1, source_target_pairs={{0,16},{8,24},{16,32},{24,40},{32,48},{40,56},{48,64},{56,72},{64,... | collective-permute-start | bytes 835592 | tf_op jit(solution)/shard_map/ppermute | solution.py:12
  56.0 4.0 collective-permute-done.3
  60.1 12.8 %collective-permute-start.4 = (f32[4,136,128]{2,1,0:T(8,128)S(1)}, f32[4,136,128]{2,1,0:T(8,128)S(1)}, u32[]{:S(2)}, u32[]{:S(2)}) collective-permute-start(f32[4,136,128]{2,1,0:T(8,128)S(1)} %pad_maximum_fusion.8), channel_id=1, source_target_pairs={{0,32},{8,40},{16,48},{24,56},{32,64},{40,72},{48,80},{56,88},{64,... | collective-permute-start | bytes 835592 | tf_op jit(solution)/shard_map/ppermute | solution.py:12
  72.9 4.7 collective-permute-done.4
  77.7 6.3 %collective-permute-start.5 = (f32[4,136,128]{2,1,0:T(8,128)S(1)}, f32[4,136,128]{2,1,0:T(8,128)S(1)}, u32[]{:S(2)}, u32[]{:S(2)}) collective-permute-start(f32[4,136,128]{2,1,0:T(8,128)S(1)} %pad_maximum_fusion.9), channel_id=1, source_target_pairs={{0,64},{8,72},{16,80},{24,88},{32,96},{40,104},{48,112},{56,120},{... | collective-permute-start | bytes 835592 | tf_op jit(solution)/shard_map/ppermute | solution.py:12
  84.2 4.3 collective-permute-done.5
  88.5 24.3 %collective-permute-start.6 = (f32[4,136,128]{2,1,0:T(8,128)S(1)}, f32[4,136,128]{2,1,0:T(8,128)S(1)}, u32[]{:S(2)}, u32[]{:S(2)}) collective-permute-start(f32[4,136,128]{2,1,0:T(8,128)S(1)} %pad_maximum_fusion.10), channel_id=1, source_target_pairs={{0,128},{8,136},{16,144},{24,152},{32,160},{40,168},{48,176},{56,1... | collective-permute-start | bytes 835592 | tf_op jit(solution)/shard_map/ppermute | solution.py:12
  113.6 4.9 %collective-permute-done.6 = f32[4,136,128]{2,1,0:T(8,128)S(1)} collective-permute-done((f32[4,136,128]{2,1,0:T(8,128)S(1)}, f32[4,136,128]{2,1,0:T(8,128)S(1)}, u32[]{:S(2)}, u32[]{:S(2)}) %collective-permute-start.6) | collective-permute-done | bytes 278560 | tf_op jit(solution)/shard_map/ppermute | solution.py:12
  119.2 3.6 multiply_reduce_fusion.4
  122.8 1.1 fusion.75
  123.9 28.5 %all-gather.5.cloned.1.call-done = bf16[512,4096]{1,0:T(8,128)(2,1)} async-done(((bf16[512,128]{1,0:T(8,128)(2,1)}), bf16[512,4096]{1,0:T(8,128)(2,1)}) %all-gather.5.cloned.1.call-update) | async-done | bytes 4194320 | tf_op jit(solution)/shard_map/all_gather | solution.py:125
  152.5 6.0 %convolution_convert_fusion.4 = bf16[512,512]{0,1:T(8,128)(2,1)S(1)} fusion(bf16[512,4096]{1,0:T(8,128)(2,1)} %all-gather.3.cloned.1.call-done, bf16[512,4096]{1,0:T(8,128)(2,1)} %all-gather.5.cloned.1.call-done), kind=kOutput, calls=%fused_computation.70 | convolution fusion | flops 2147745792 | bytes 8912896 | tf_op jit(solution)/shard_map/dot_general | solution.py:123
  158.9 1.4 fusion.78
  160.4 1.3 collective-permute-start.7
  161.7 2.4 fusion.14
  164.1 3.1 copy.138
  167.2 4.2 collective-permute-done.7
  171.4 1.5 collective-permute-start.8
  172.8 4.5 convolution_convert_fusion
  177.3 2.6 collective-permute-done.8
  180.6 1.1 slice_add_fusion
  181.7 1.3 collective-permute-start.9
  183.0 5.8 %fusion.41 = f32[512,4,128]{0,2,1:T(8,128)S(1)} fusion(f32[4,512,512]{2,1,0:T(8,128)} %copy-done.7, f32[4,512]{1,0:T(4,128)S(1)} %bitcast.265, pred[512,512]{1,0:T(8,128)(4,1)} %copy-done.18, f32[4,512,128]{1,2,0:T(8,128)S(1)} %get-tuple-element.57, f32[4,512]{1,0:T(4,128)S(1)} %broadcast_multiply_fusion, f32[4,128]{1,0:T(4,128)S(1)} %bitcast.254, ...), kind=kOutput, calls=%fused_computation.56 | convolution fusion | flops 1616379904 | bytes 7104512 | tf_op jit(solution)/shard_map/hts,htj->hsj/dot_general | solution.py:161
  188.8 2.9 collective-permute-done.9
  191.8 1.4 collective-permute-start.10
  193.2 2.0 fusion.120
  195.2 6.3 %collective-permute-done.10 = f32[4,136,128]{2,1,0:T(8,128)S(1)} collective-permute-done((f32[4,136,128]{2,1,0:T(8,128)S(1)}, f32[4,136,128]{2,1,0:T(8,128)S(1)}, u32[]{:S(2)}, u32[]{:S(2)}) %collective-permute-start.10) | collective-permute-done | bytes 278560 | tf_op jit(solution)/shard_map/ppermute | solution.py:12
  201.6 1.3 collective-permute-start.11
  202.9 3.5 fusion.35
  206.4 10.0 %collective-permute-done.11 = f32[4,136,128]{2,1,0:T(8,128)S(1)} collective-permute-done((f32[4,136,128]{2,1,0:T(8,128)S(1)}, f32[4,136,128]{2,1,0:T(8,128)S(1)}, u32[]{:S(2)}, u32[]{:S(2)}) %collective-permute-start.11) | collective-permute-done | bytes 278560 | tf_op jit(solution)/shard_map/ppermute | solution.py:12
  216.5 1.5 collective-permute-start.12
  218.0 2.7 fusion.38
  220.8 10.7 %collective-permute-done.12 = f32[4,136,128]{2,1,0:T(8,128)S(1)} collective-permute-done((f32[4,136,128]{2,1,0:T(8,128)S(1)}, f32[4,136,128]{2,1,0:T(8,128)S(1)}, u32[]{:S(2)}, u32[]{:S(2)}) %collective-permute-start.12) | collective-permute-done | bytes 278560 | tf_op jit(solution)/shard_map/ppermute | solution.py:12
  232.9 2.2 add_convert_fusion
  236.5 1.4 copy.98
  237.9 1.4 collective-permute-start.13
  239.3 2.0 fusion.51
  242.3 1.5 pad_maximum_fusion.2
  244.3 1.2 copy.99
  245.5 1.6 pad_maximum_fusion
  247.9 8.4 %multiply_reduce_fusion.3 = (bf16[3,512]{1,0:T(4,128)(2,1)S(1)}, bf16[3,512]{1,0:T(4,128)(2,1)S(1)}, bf16[3,512]{1,0:T(4,128)(2,1)S(1)}, bf16[3,512]{1,0:T(4,128)(2,1)S(1)}, bf16[3,512,512]{1,2,0:T(8,128)(2,1)}) fusion(f32[3,515,512]{1,2,0:T(8,128)S(1)} %copy-done.1, f32[1,512,512]{1,2,0:T(8,128)S(1)} %bitcast.225, f32[1,512,512]{1,2,0:T(8,128)S(1)} %bitcast.218, ...), kind=kLoop, calls=%fused_computation.19 | loop fusion | flops 14149632 | bytes 26775552 | tf_op jit(solution)/shard_map/reduce_sum | solution.py:177
  256.3 11.3 %concatenate.50 = bf16[2061,512]{1,0:T(8,128)(2,1)} concatenate(bf16[2048,512]{1,0:T(8,128)(2,1)} %bitcast.226, bf16[12,512]{1,0:T(8,128)(2,1)S(1)} %convert_element_type.123, bf16[1,512]{1,0:T(2,128)(2,1)S(1)} %bitcast.268), dimensions={0} | concatenate | bytes 4220928 | tf_op jit(solution)/shard_map/concatenate | solution.py:194
  267.7 16.4 %all-to-all-start = ((bf16[32,512,128]{2,1,0:T(8,128)(2,1)}), bf16[32,512,128]{2,1,0:T(8,128)(2,1)}, u32[]{:S(2)}, u32[]{:S(2)}) async-start(bf16[32,512,128]{2,1,0:T(8,128)(2,1)} %bitcast.222), calls=%async_computation.1 | async-start | bytes 8388608 | tf_op jit(solution)/shard_map/all_to_all | solution.py:203
  285.6 1.0 copy.100
  286.6 1.0 copy.101
  287.6 1.0 copy.102
  288.6 184.5 %all-reduce.2.cloned.1.call-done = bf16[2061,512]{1,0:T(8,128)(2,1)} async-done(((bf16[2061,512]{1,0:T(8,128)(2,1)}), bf16[2061,512]{1,0:T(8,128)(2,1)}) %all-reduce.2.cloned.1.call-update) | async-done | bytes 2110480 | tf_op jit(solution)/shard_map/psum | solution.py:202
  474.4 4.2 slice.316
  478.6 1.3 slice.317
  479.9 3.5 convert_reduce_fusion
  (135 shorter events, 14.5 us)
Async XLA Ops:
  7.2 8.4 %copy-start.21 = (f32[3,4,512]{2,1,0:T(4,128)S(1)}, f32[3,4,512]{2,1,0:T(4,128)}, u32[]{:S(2)}) copy-start(f32[3,4,512]{2,1,0:T(4,128)} %param.13) | copy-start | bytes 73732
  7.2 8.4 %copy-start.22 = (f32[4,512]{1,0:T(4,128)S(1)}, f32[4,512]{1,0:T(4,128)}, u32[]{:S(2)}) copy-start(f32[4,512]{1,0:T(4,128)} %param.16) | copy-start | bytes 24580
  7.2 10.2 %copy-start.23 = (s32[4,512]{1,0:T(4,128)S(1)}, s32[4,512]{1,0:T(4,128)}, u32[]{:S(2)}) copy-start(s32[4,512]{1,0:T(4,128)} %param.14) | copy-start | bytes 24580
  7.2 116.7 %all-gather.3.cloned.1.call-start = ((), (), s32[]{:S(2)}) async-start(), calls=%async_computation.2 | async-start | bytes 4718592 | tf_op jit(solution)/shard_map/all_gather | solution.py:121
  7.9 144.5 %all-gather.5.cloned.1.call-start = ((), (), s32[]{:S(2)}) async-start(), calls=%async_computation.3 | async-start | bytes 4325376 | tf_op jit(solution)/shard_map/all_gather | solution.py:125
  11.9 11.8 %collective-permute-start = (bf16[3,3,512]{1,2,0:T(8,128)(2,1)S(1)}, bf16[3,3,512]{1,2,0:T(8,128)(2,1)S(1)}, u32[]{:S(2)}, u32[]{:S(2)}) collective-permute-start(bf16[3,3,512]{1,2,0:T(8,128)(2,1)S(1)} %pad_maximum_fusion.5), channel_id=1, source_target_pairs={{0,8},{8,16},{16,24},{24,32},{32,40},{40,48},{48,56},{56,64},{64,7... | collective-permute-start | bytes 27656 | tf_op jit(solution)/shard_map/ppermute | solution.py:12
  15.5 252.2 %reduce-scatter.2.cloned.1.call-start = ((), (), s32[]{:S(2)}) async-start(), calls=%async_computation.4 | async-start | bytes 4718592 | tf_op jit(solution)/shard_map/reduce_scatter | solution.py:118
  24.6 3.8 copy-start
  24.6 3.9 copy-start.25
  29.6 0.8 copy-start.15
  29.6 129.3 %copy-start.9 = (bf16[512,512]{0,1:T(8,128)(2,1)}, bf16[512,512]{0,1:T(8,128)(2,1)S(1)}, u32[]{:S(2)}) copy-start(bf16[512,512]{0,1:T(8,128)(2,1)S(1)} %get-tuple-element.58) | copy-start | bytes 1572868
  31.8 9.4 %collective-permute-start.1 = (f32[4,136,128]{2,1,0:T(8,128)S(1)}, f32[4,136,128]{2,1,0:T(8,128)S(1)}, u32[]{:S(2)}, u32[]{:S(2)}) collective-permute-start(f32[4,136,128]{2,1,0:T(8,128)S(1)} %pad_maximum_fusion.4), channel_id=1, source_target_pairs={{0,8},{8,16},{16,24},{24,32},{32,40},{40,48},{48,56},{56,64},{64,7... | collective-permute-start | bytes 835592 | tf_op jit(solution)/shard_map/ppermute | solution.py:12
  41.3 8.7 %collective-permute-start.2 = (f32[4,136,128]{2,1,0:T(8,128)S(1)}, f32[4,136,128]{2,1,0:T(8,128)S(1)}, u32[]{:S(2)}, u32[]{:S(2)}) collective-permute-start(f32[4,136,128]{2,1,0:T(8,128)S(1)} %collective-permute-done.1), channel_id=1, source_target_pairs={{0,8},{8,16},{16,24},{24,32},{32,40},{40,48},{48,56},{56,64},{64,7... | collective-permute-start | bytes 835592 | tf_op jit(solution)/shard_map/ppermute | solution.py:12
  50.0 10.1 %collective-permute-start.3 = (f32[4,136,128]{2,1,0:T(8,128)S(1)}, f32[4,136,128]{2,1,0:T(8,128)S(1)}, u32[]{:S(2)}, u32[]{:S(2)}) collective-permute-start(f32[4,136,128]{2,1,0:T(8,128)S(1)} %pad_maximum_fusion.7), channel_id=1, source_target_pairs={{0,16},{8,24},{16,32},{24,40},{32,48},{40,56},{48,64},{56,72},{64,... | collective-permute-start | bytes 835592 | tf_op jit(solution)/shard_map/ppermute | solution.py:12
  60.1 17.5 %collective-permute-start.4 = (f32[4,136,128]{2,1,0:T(8,128)S(1)}, f32[4,136,128]{2,1,0:T(8,128)S(1)}, u32[]{:S(2)}, u32[]{:S(2)}) collective-permute-start(f32[4,136,128]{2,1,0:T(8,128)S(1)} %pad_maximum_fusion.8), channel_id=1, source_target_pairs={{0,32},{8,40},{16,48},{24,56},{32,64},{40,72},{48,80},{56,88},{64,... | collective-permute-start | bytes 835592 | tf_op jit(solution)/shard_map/ppermute | solution.py:12
  77.7 10.7 %collective-permute-start.5 = (f32[4,136,128]{2,1,0:T(8,128)S(1)}, f32[4,136,128]{2,1,0:T(8,128)S(1)}, u32[]{:S(2)}, u32[]{:S(2)}) collective-permute-start(f32[4,136,128]{2,1,0:T(8,128)S(1)} %pad_maximum_fusion.9), channel_id=1, source_target_pairs={{0,64},{8,72},{16,80},{24,88},{32,96},{40,104},{48,112},{56,120},{... | collective-permute-start | bytes 835592 | tf_op jit(solution)/shard_map/ppermute | solution.py:12
  84.1 35.0 %copy-start.18 = (pred[512,512]{1,0:T(8,128)(4,1)}, pred[512,512]{1,0:T(8,128)(4,1)S(1)}, u32[]{:S(2)}) copy-start(pred[512,512]{1,0:T(8,128)(4,1)S(1)} %iota_compare_fusion.4) | copy-start | bytes 786436
  88.5 30.0 %collective-permute-start.6 = (f32[4,136,128]{2,1,0:T(8,128)S(1)}, f32[4,136,128]{2,1,0:T(8,128)S(1)}, u32[]{:S(2)}, u32[]{:S(2)}) collective-permute-start(f32[4,136,128]{2,1,0:T(8,128)S(1)} %pad_maximum_fusion.10), channel_id=1, source_target_pairs={{0,128},{8,136},{16,144},{24,152},{32,160},{40,168},{48,176},{56,1... | collective-permute-start | bytes 835592 | tf_op jit(solution)/shard_map/ppermute | solution.py:12
  113.5 5.6 %copy-start.7 = (f32[4,512,512]{2,1,0:T(8,128)}, f32[4,512,512]{2,1,0:T(8,128)S(1)}, u32[]{:S(2)}) copy-start(f32[4,512,512]{2,1,0:T(8,128)S(1)} %fusion.96) | copy-start | bytes 12582916
  118.5 4.3 copy-start.12
  119.2 3.7 copy-start.20
  122.8 70.4 %copy-start.2 = (f32[4,512,128]{1,2,0:T(8,128)}, f32[4,512,128]{1,2,0:T(8,128)S(1)}, u32[]{:S(2)}) copy-start(f32[4,512,128]{1,2,0:T(8,128)S(1)} %get-tuple-element.57) | copy-start | bytes 3145732
  152.4 9.2 %copy-start.24 = (bf16[512,4096]{1,0:T(8,128)(2,1)S(1)}, bf16[512,4096]{1,0:T(8,128)(2,1)}, u32[]{:S(2)}) copy-start(bf16[512,4096]{1,0:T(8,128)(2,1)} %all-gather.3.cloned.1.call-done) | copy-start | bytes 12582916
  158.4 34.8 %copy-start.5 = (bf16[512,512]{0,1:T(8,128)(2,1)}, bf16[512,512]{0,1:T(8,128)(2,1)S(1)}, u32[]{:S(2)}) copy-start(bf16[512,512]{0,1:T(8,128)(2,1)S(1)} %convolution_convert_fusion.4) | copy-start | bytes 1572868
  158.4 3.3 copy-start.11
  160.4 11.0 %collective-permute-start.7 = (f32[4,136,128]{2,1,0:T(8,128)S(1)}, f32[4,136,128]{2,1,0:T(8,128)S(1)}, u32[]{:S(2)}, u32[]{:S(2)}) collective-permute-start(f32[4,136,128]{2,1,0:T(8,128)S(1)} %pad_maximum_fusion.3), channel_id=1, source_target_pairs={{8,0},{16,8},{24,16},{32,24},{40,32},{48,40},{56,48},{64,56},{72,6... | collective-permute-start | bytes 835592 | tf_op jit(solution)/shard_map/ppermute | solution.py:12
  164.1 8.8 %copy-start.8 = (bf16[512,4096]{1,0:T(8,128)(2,1)S(1)}, bf16[512,4096]{1,0:T(8,128)(2,1)}, u32[]{:S(2)}) copy-start(bf16[512,4096]{1,0:T(8,128)(2,1)} %all-gather.5.cloned.1.call-done) | copy-start | bytes 12582916
  171.4 8.5 %copy-start.17 = (f32[4,136,128]{2,1,0:T(8,128)}, f32[4,136,128]{2,1,0:T(8,128)S(1)}, u32[]{:S(2)}) copy-start(f32[4,136,128]{2,1,0:T(8,128)S(1)} %collective-permute-done.7) | copy-start | bytes 835588
  171.4 8.5 %collective-permute-start.8 = (f32[4,136,128]{2,1,0:T(8,128)S(1)}, f32[4,136,128]{2,1,0:T(8,128)}, u32[]{:S(2)}, u32[]{:S(2)}) collective-permute-start(f32[4,136,128]{2,1,0:T(8,128)S(1)} %collective-permute-done.7), channel_id=1, source_target_pairs={{8,0},{16,8},{24,16},{32,24},{40,32},{48,40},{56,48},{64,56},{72,6... | collective-permute-start | bytes 835592 | tf_op jit(solution)/shard_map/ppermute | solution.py:12
  181.7 9.9 %collective-permute-start.9 = (f32[4,136,128]{2,1,0:T(8,128)S(1)}, f32[4,136,128]{2,1,0:T(8,128)S(1)}, u32[]{:S(2)}, u32[]{:S(2)}) collective-permute-start(f32[4,136,128]{2,1,0:T(8,128)S(1)} %pad_maximum_fusion.11), channel_id=1, source_target_pairs={{16,0},{24,8},{32,16},{40,24},{48,32},{56,40},{64,48},{72,56},{80,... | collective-permute-start | bytes 835592 | tf_op jit(solution)/shard_map/ppermute | solution.py:12
  191.8 11.2 %copy-start.16 = (bf16[512,512]{0,1:T(8,128)(2,1)S(1)}, bf16[512,512]{0,1:T(8,128)(2,1)}, u32[]{:S(2)}) copy-start(bf16[512,512]{0,1:T(8,128)(2,1)} %copy-done.15) | copy-start | bytes 1572868
  191.8 11.2 %copy-start.19 = (pred[512,512]{1,0:T(8,128)(4,1)S(1)}, pred[512,512]{1,0:T(8,128)(4,1)}, u32[]{:S(2)}) copy-start(pred[512,512]{1,0:T(8,128)(4,1)} %copy-done.18) | copy-start | bytes 786436
  191.8 9.8 %collective-permute-start.10 = (f32[4,136,128]{2,1,0:T(8,128)S(1)}, f32[4,136,128]{2,1,0:T(8,128)S(1)}, u32[]{:S(2)}, u32[]{:S(2)}) collective-permute-start(f32[4,136,128]{2,1,0:T(8,128)S(1)} %pad_maximum_fusion.12), channel_id=1, source_target_pairs={{32,0},{40,8},{48,16},{56,24},{64,32},{72,40},{80,48},{88,56},{96,... | collective-permute-start | bytes 835592 | tf_op jit(solution)/shard_map/ppermute | solution.py:12
  201.6 14.8 %collective-permute-start.11 = (f32[4,136,128]{2,1,0:T(8,128)S(1)}, f32[4,136,128]{2,1,0:T(8,128)S(1)}, u32[]{:S(2)}, u32[]{:S(2)}) collective-permute-start(f32[4,136,128]{2,1,0:T(8,128)S(1)} %pad_maximum_fusion.13), channel_id=1, source_target_pairs={{64,0},{72,8},{80,16},{88,24},{96,32},{104,40},{112,48},{120,56},{... | collective-permute-start | bytes 835592 | tf_op jit(solution)/shard_map/ppermute | solution.py:12
  202.9 15.1 %copy-start.10 = (bf16[512,512]{0,1:T(8,128)(2,1)S(1)}, bf16[512,512]{0,1:T(8,128)(2,1)}, u32[]{:S(2)}) copy-start(bf16[512,512]{0,1:T(8,128)(2,1)} %copy-done.9) | copy-start | bytes 1572868
  216.5 15.0 %collective-permute-start.12 = (f32[4,136,128]{2,1,0:T(8,128)S(1)}, f32[4,136,128]{2,1,0:T(8,128)S(1)}, u32[]{:S(2)}, u32[]{:S(2)}) collective-permute-start(f32[4,136,128]{2,1,0:T(8,128)S(1)} %pad_maximum_fusion.14), channel_id=1, source_target_pairs={{128,0},{136,8},{144,16},{152,24},{160,32},{168,40},{176,48},{184,... | collective-permute-start | bytes 835592 | tf_op jit(solution)/shard_map/ppermute | solution.py:12
  231.5 1.3 copy-start.3
  231.5 1.4 copy-start.6
  231.5 1.4 copy-start.13
  237.9 3.5 copy-start.14
  237.9 6.4 %collective-permute-start.13 = (f32[3,3,512]{2,1,0:T(4,128)S(1)}, f32[3,3,512]{2,1,0:T(4,128)S(1)}, u32[]{:S(2)}, u32[]{:S(2)}) collective-permute-start(f32[3,3,512]{2,1,0:T(4,128)S(1)} %copy.98), channel_id=1, source_target_pairs={{8,0},{16,8},{24,16},{32,24},{40,32},{48,40},{56,48},{64,56},{72,6... | collective-permute-start | bytes 55304 | tf_op jit(solution)/shard_map/ppermute | solution.py:12
  245.5 2.3 copy-start.1
  267.7 212.3 %all-to-all-start = ((bf16[32,512,128]{2,1,0:T(8,128)(2,1)}), bf16[32,512,128]{2,1,0:T(8,128)(2,1)}, u32[]{:S(2)}, u32[]{:S(2)}) async-start(bf16[32,512,128]{2,1,0:T(8,128)(2,1)} %bitcast.222), calls=%async_computation.1 | async-start | bytes 8388608 | tf_op jit(solution)/shard_map/all_to_all | solution.py:203
  284.1 1.4 copy-start.4
  284.1 189.0 %all-reduce.2.cloned.1.call-start = ((), (), s32[]{:S(2)}) async-start(), calls=%async_computation.5 | async-start | bytes 4227072 | tf_op jit(solution)/shard_map/psum | solution.py:202
Sparse Core Ops, SparseCore 0:
  9.8 36.5 all-gather.2
  48.9 103.5 all-gather.4
  177.4 35.0 reduce-scatter.1
  288.1 184.9 all-reduce.1
where the time goes:
time: 497 us; the launch traced here: 490 us
  waiting for transfers between devices  283 us (57%)
  starting transfers between devices  87.9 us (18%)
  matrix products  44.2 us (9%)
  local copies, waits for them, and re-layouts  34.9 us (7%)
  other arithmetic  25.7 us (5%)
  between operations  14.9 us (3%)
    psum x1, waiting for transfers between devices, on_device(): summed = lax.psum(packed, 'seq').astype(jnp.float32)  184 us
    ppermute x14, starting transfers between devices, shifted(): return lax.ppermute(x, axis, pairs)  71.4 us
    ppermute x14, waiting for transfers between devices, shifted(): return lax.ppermute(x, axis, pairs)  68.3 us
    all_gather x1, waiting for transfers between devices, on_device(): lax.all_gather(out_weight, 'seq', axis=1, tiled=True)  28.5 us
    all_to_all x1, starting transfers between devices, on_device(): weight_parts = lax.all_to_all(weight_parts, 'seq', 0, 0, tiled=True)  16.4 us
    concatenate x1, local copies, waits for them, and re-layouts, on_device(): jnp.concatenate([table_terms.astype(jnp.bfloat16).reshape(table_rows, fea...  11.3 us
  transfers between devices with their start and end apart: 19, of which 16 were waited for; matrix products, arithmetic and copies ran while one was open for 19% of the time, Pallas kernels for 0%

commit v1 on v0

--- a/solution.py
+++ b/solution.py
@@ -4,6 +4,11 @@
 from jax.sharding import PartitionSpec as P
 
 HIGHEST = lax.Precision.HIGHEST
+
+
+def add_all(x, mesh_axis):
+    parts = lax.all_gather(x, mesh_axis)
+    return jnp.sum(parts, axis=0)
 
 
 def shifted(x, axis, by):
@@ -199,7 +204,7 @@
         ]
     )
     packed, layer_out, weight_parts = lax.optimization_barrier((packed, layer_out, weight_parts))
-    summed = lax.psum(packed, "seq").astype(jnp.float32)
+    summed = add_all(packed, "seq").astype(jnp.float32)
     weight_parts = lax.all_to_all(weight_parts, "seq", 0, 0, tiled=True)
     grad_weight = jnp.sum(weight_parts.astype(jnp.float32), axis=0)
     grad_tables = summed[:table_rows].reshape(2, buckets, feat_width)

time: 497 us -> 818 us (1.65)
  waiting for transfers between devices: 283 us -> 584 us
  other arithmetic: 25.7 us -> 47.7 us
    all_gather x0 -> x1, waiting for transfers between devices: none -> 366 us  [add_all(): parts = lax.all_gather(x, mesh_axis)]
    psum x1 -> x0, waiting for transfers between devices: 184 us -> none  [on_device(): summed = lax.psum(packed, 'seq').astype(jnp.float32)]
    all_to_all x1, waiting for transfers between devices: 0.01 us -> 121 us  [on_device(): weight_parts = lax.all_to_all(weight_parts, 'seq', 0, 0, tiled=True)]
    reduce_sum x0 -> x1, other arithmetic: none -> 21.9 us  [add_all(): return jnp.sum(parts, axis=0)]
  transfers between devices with their start and end apart: 19 -> 19, of which waited for: 16 -> 17; matrix products, arithmetic and copies ran while one was open for 19% -> 11% of each run, Pallas kernels for 0% -> 0%
where the time goes in v1:
time: 818 us; the launch traced here: 810 us
  waiting for transfers between devices  584 us (71%)
  starting transfers between devices  88.4 us (11%)
  other arithmetic  47.7 us (6%)
  matrix products  44.2 us (5%)
  local copies, waits for them, and re-layouts  31.1 us (4%)
  between operations  14.9 us (2%)
    all_gather x1, waiting for transfers between devices, add_all(): parts = lax.all_gather(x, mesh_axis)  366 us
    all_to_all x1, waiting for transfers between devices, on_device(): weight_parts = lax.all_to_all(weight_parts, 'seq', 0, 0, tiled=True)  121 us
    ppermute x14, starting transfers between devices, shifted(): return lax.ppermute(x, axis, pairs)  71.4 us
    ppermute x14, waiting for transfers between devices, shifted(): return lax.ppermute(x, axis, pairs)  68.1 us
    all_gather x1, waiting for transfers between devices, on_device(): lax.all_gather(out_weight, 'seq', axis=1, tiled=True)  28.5 us
    reduce_sum x1, other arithmetic, add_all(): return jnp.sum(parts, axis=0)  21.9 us
    all_to_all x1, starting transfers between devices, on_device(): weight_parts = lax.all_to_all(weight_parts, 'seq', 0, 0, tiled=True)  16.9 us
  transfers between devices with their start and end apart: 19, of which 17 were waited for; matrix products, arithmetic and copies ran while one was open for 11% of the time, Pallas kernels for 0%

profile of v1, /device:TPU:2, one launch (start us, length us, event | category | flops | bytes accessed | tf_op | source)
XLA Modules:
  0.0 810.4 jit_solution(15780592282849066111)
XLA Ops:
  8.0 1.3 copy.79
  9.2 1.3 copy.80
  10.5 1.3 copy.81
  11.9 3.5 collective-permute-start
  15.5 1.2 reduce-window.6
  17.5 2.3 fusion.58
  19.8 4.0 collective-permute-done
  24.6 3.7 multiply_add_fusion
  28.5 1.1 fusion.64
  30.4 1.3 fusion.81
  31.8 4.4 collective-permute-start.1
  36.2 5.0 collective-permute-done.1
  41.3 4.4 collective-permute-start.2
  45.7 4.3 collective-permute-done.2
  50.0 6.0 collective-permute-start.3
  56.0 4.0 collective-permute-done.3
  60.1 12.8 %collective-permute-start.4 = (f32[4,136,128]{2,1,0:T(8,128)S(1)}, f32[4,136,128]{2,1,0:T(8,128)S(1)}, u32[]{:S(2)}, u32[]{:S(2)}) collective-permute-start(f32[4,136,128]{2,1,0:T(8,128)S(1)} %pad_maximum_fusion.8), channel_id=1, source_target_pairs={{0,32},{8,40},{16,48},{24,56},{32,64},{40,72},{48,80},{56,88},{64,... | collective-permute-start | bytes 835592 | tf_op jit(solution)/shard_map/ppermute | solution.py:17
  72.9 4.7 collective-permute-done.4
  77.7 6.4 collective-permute-start.5
  84.2 4.3 collective-permute-done.5
  88.5 24.3 %collective-permute-start.6 = (f32[4,136,128]{2,1,0:T(8,128)S(1)}, f32[4,136,128]{2,1,0:T(8,128)S(1)}, u32[]{:S(2)}, u32[]{:S(2)}) collective-permute-start(f32[4,136,128]{2,1,0:T(8,128)S(1)} %pad_maximum_fusion.10), channel_id=1, source_target_pairs={{0,128},{8,136},{16,144},{24,152},{32,160},{40,168},{48,176},{56,1... | collective-permute-start | bytes 835592 | tf_op jit(solution)/shard_map/ppermute | solution.py:17
  113.6 4.9 collective-permute-done.6
  119.2 3.6 multiply_reduce_fusion.4
  122.8 1.1 fusion.75
  123.9 28.5 %all-gather.8.cloned.1.call-done = bf16[512,4096]{1,0:T(8,128)(2,1)} async-done(((bf16[512,128]{1,0:T(8,128)(2,1)}), bf16[512,4096]{1,0:T(8,128)(2,1)}) %all-gather.8.cloned.1.call-update) | async-done | bytes 4194320 | tf_op jit(solution)/shard_map/all_gather | solution.py:130
  152.4 6.0 convolution_convert_fusion.4
  158.9 1.4 fusion.78
  160.4 1.3 collective-permute-start.7
  161.7 2.4 fusion.14
  164.1 3.2 copy.138
  167.3 4.0 collective-permute-done.7
  171.2 1.5 collective-permute-start.8
  172.7 4.5 convolution_convert_fusion
  177.3 2.5 collective-permute-done.8
  180.5 1.1 slice_add_fusion
  181.6 1.3 collective-permute-start.9
  182.9 5.8 fusion.41
  188.7 2.9 collective-permute-done.9
  191.6 1.4 collective-permute-start.10
  193.1 2.0 fusion.120
  195.1 6.3 collective-permute-done.10
  201.5 1.3 collective-permute-start.11
  202.8 3.5 fusion.35
  206.3 9.9 %collective-permute-done.11 = f32[4,136,128]{2,1,0:T(8,128)S(1)} collective-permute-done((f32[4,136,128]{2,1,0:T(8,128)S(1)}, f32[4,136,128]{2,1,0:T(8,128)S(1)}, u32[]{:S(2)}, u32[]{:S(2)}) %collective-permute-start.11) | collective-permute-done | bytes 278560 | tf_op jit(solution)/shard_map/ppermute | solution.py:17
  216.3 1.5 collective-permute-start.12
  217.8 2.7 fusion.38
  220.6 10.8 %collective-permute-done.12 = f32[4,136,128]{2,1,0:T(8,128)S(1)} collective-permute-done((f32[4,136,128]{2,1,0:T(8,128)S(1)}, f32[4,136,128]{2,1,0:T(8,128)S(1)}, u32[]{:S(2)}, u32[]{:S(2)}) %collective-permute-start.12) | collective-permute-done | bytes 278560 | tf_op jit(solution)/shard_map/ppermute | solution.py:17
  232.8 2.2 add_convert_fusion
  236.3 1.4 copy.98
  237.7 1.4 collective-permute-start.13
  239.1 2.0 fusion.52
  242.1 1.5 pad_maximum_fusion.2
  244.2 1.2 copy.99
  245.4 1.6 pad_maximum_fusion
  247.8 8.4 %multiply_reduce_fusion.3 = (bf16[3,512]{1,0:T(4,128)(2,1)S(1)}, bf16[3,512]{1,0:T(4,128)(2,1)S(1)}, bf16[3,512]{1,0:T(4,128)(2,1)S(1)}, bf16[3,512]{1,0:T(4,128)(2,1)S(1)}, bf16[3,512,512]{1,2,0:T(8,128)(2,1)}) fusion(f32[3,515,512]{1,2,0:T(8,128)S(1)} %copy-done.1, f32[1,512,512]{1,2,0:T(8,128)S(1)} %bitcast.226, f32[1,512,512]{1,2,0:T(8,128)S(1)} %bitcast.219, ...), kind=kLoop, calls=%fused_computation.19 | loop fusion | flops 14149632 | bytes 26775552 | tf_op jit(solution)/shard_map/reduce_sum | solution.py:182
  256.2 11.3 %concatenate.50 = bf16[2061,512]{1,0:T(8,128)(2,1)} concatenate(bf16[2048,512]{1,0:T(8,128)(2,1)} %bitcast.228, bf16[12,512]{1,0:T(8,128)(2,1)S(1)} %convert_element_type.125, bf16[1,512]{1,0:T(2,128)(2,1)S(1)} %bitcast.270), dimensions={0} | concatenate | bytes 4220928 | tf_op jit(solution)/shard_map/concatenate | solution.py:199
  267.6 16.9 %all-to-all-start = ((bf16[32,512,128]{2,1,0:T(8,128)(2,1)}), bf16[32,512,128]{2,1,0:T(8,128)(2,1)}, u32[]{:S(2)}, u32[]{:S(2)}) async-start(bf16[32,512,128]{2,1,0:T(8,128)(2,1)} %bitcast.223), calls=%async_computation.1 | async-start | bytes 8388608 | tf_op jit(solution)/shard_map/all_to_all | solution.py:208
  284.6 1.0 copy.102
  285.6 1.0 copy.101
  287.6 120.8 %all-to-all-done = bf16[32,512,128]{2,1,0:T(8,128)(2,1)} async-done(((bf16[32,512,128]{2,1,0:T(8,128)(2,1)}), bf16[32,512,128]{2,1,0:T(8,128)(2,1)}, u32[]{:S(2)}, u32[]{:S(2)}) %all-to-all-start) | async-done | bytes 4194336 | tf_op jit(solution)/shard_map/all_to_all | solution.py:208
  408.5 3.5 convert_reduce_fusion
  412.0 365.9 %all-gather.10.cloned.1.call-done = bf16[32,2061,512]{2,1,0:T(8,128)(2,1)} async-done(((bf16[1,2061,512]{2,1,0:T(8,128)(2,1)}), bf16[32,2061,512]{2,1,0:T(8,128)(2,1)}) %all-gather.10.cloned.1.call-update) | async-done | bytes 67534864 | tf_op jit(solution)/shard_map/all_gather | solution.py:10
  777.8 21.9 %reduce_sum.91 = bf16[2061,512]{1,0:T(8,128)(2,1)S(1)} reduce(bf16[32,2061,512]{2,1,0:T(8,128)(2,1)} %all-gather.10.cloned.1.call-done, bf16[]{:T(256)} %constant.15.clone.1), dimensions={0}, to_apply=%region_10.11 | reduce | flops 32712192 | bytes 69645312 | tf_op jit(solution)/shard_map/reduce_sum | solution.py:11
  800.4 2.6 slice.316
  (136 shorter events, 14.2 us)
Async XLA Ops:
  7.2 8.4 %copy-start.22 = (f32[4,512]{1,0:T(4,128)S(1)}, f32[4,512]{1,0:T(4,128)}, u32[]{:S(2)}) copy-start(f32[4,512]{1,0:T(4,128)} %param.16) | copy-start | bytes 24580
  7.2 10.2 %copy-start.21 = (f32[3,4,512]{2,1,0:T(4,128)S(1)}, f32[3,4,512]{2,1,0:T(4,128)}, u32[]{:S(2)}) copy-start(f32[3,4,512]{2,1,0:T(4,128)} %param.13) | copy-start | bytes 73732
  7.2 10.2 %copy-start.23 = (s32[4,512]{1,0:T(4,128)S(1)}, s32[4,512]{1,0:T(4,128)}, u32[]{:S(2)}) copy-start(s32[4,512]{1,0:T(4,128)} %param.14) | copy-start | bytes 24580
  7.2 116.7 %all-gather.6.cloned.1.call-start = ((), (), s32[]{:S(2)}) async-start(), calls=%async_computation.2 | async-start | bytes 4718592 | tf_op jit(solution)/shard_map/all_gather | solution.py:126
  7.9 144.5 %all-gather.8.cloned.1.call-start = ((), (), s32[]{:S(2)}) async-start(), calls=%async_computation.3 | async-start | bytes 4325376 | tf_op jit(solution)/shard_map/all_gather | solution.py:130
  11.9 11.8 %collective-permute-start = (bf16[3,3,512]{1,2,0:T(8,128)(2,1)S(1)}, bf16[3,3,512]{1,2,0:T(8,128)(2,1)S(1)}, u32[]{:S(2)}, u32[]{:S(2)}) collective-permute-start(bf16[3,3,512]{1,2,0:T(8,128)(2,1)S(1)} %pad_maximum_fusion.5), channel_id=1, source_target_pairs={{0,8},{8,16},{16,24},{24,32},{32,40},{40,48},{48,56},{56,64},{64,7... | collective-permute-start | bytes 27656 | tf_op jit(solution)/shard_map/ppermute | solution.py:17
  15.5 252.1 %reduce-scatter.2.cloned.1.call-start = ((), (), s32[]{:S(2)}) async-start(), calls=%async_computation.4 | async-start | bytes 4718592 | tf_op jit(solution)/shard_map/reduce_scatter | solution.py:123
  24.6 3.8 copy-start
  24.6 3.9 copy-start.25
  29.6 0.8 copy-start.15
  29.6 129.3 %copy-start.9 = (bf16[512,512]{0,1:T(8,128)(2,1)}, bf16[512,512]{0,1:T(8,128)(2,1)S(1)}, u32[]{:S(2)}) copy-start(bf16[512,512]{0,1:T(8,128)(2,1)S(1)} %get-tuple-element.58) | copy-start | bytes 1572868
  31.8 9.4 %collective-permute-start.1 = (f32[4,136,128]{2,1,0:T(8,128)S(1)}, f32[4,136,128]{2,1,0:T(8,128)S(1)}, u32[]{:S(2)}, u32[]{:S(2)}) collective-permute-start(f32[4,136,128]{2,1,0:T(8,128)S(1)} %pad_maximum_fusion.4), channel_id=1, source_target_pairs={{0,8},{8,16},{16,24},{24,32},{32,40},{40,48},{48,56},{56,64},{64,7... | collective-permute-start | bytes 835592 | tf_op jit(solution)/shard_map/ppermute | solution.py:17
  41.3 8.7 %collective-permute-start.2 = (f32[4,136,128]{2,1,0:T(8,128)S(1)}, f32[4,136,128]{2,1,0:T(8,128)S(1)}, u32[]{:S(2)}, u32[]{:S(2)}) collective-permute-start(f32[4,136,128]{2,1,0:T(8,128)S(1)} %collective-permute-done.1), channel_id=1, source_target_pairs={{0,8},{8,16},{16,24},{24,32},{32,40},{40,48},{48,56},{56,64},{64,7... | collective-permute-start | bytes 835592 | tf_op jit(solution)/shard_map/ppermute | solution.py:17
  50.0 10.1 %collective-permute-start.3 = (f32[4,136,128]{2,1,0:T(8,128)S(1)}, f32[4,136,128]{2,1,0:T(8,128)S(1)}, u32[]{:S(2)}, u32[]{:S(2)}) collective-permute-start(f32[4,136,128]{2,1,0:T(8,128)S(1)} %pad_maximum_fusion.7), channel_id=1, source_target_pairs={{0,16},{8,24},{16,32},{24,40},{32,48},{40,56},{48,64},{56,72},{64,... | collective-permute-start | bytes 835592 | tf_op jit(solution)/shard_map/ppermute | solution.py:17
  60.1 17.5 %collective-permute-start.4 = (f32[4,136,128]{2,1,0:T(8,128)S(1)}, f32[4,136,128]{2,1,0:T(8,128)S(1)}, u32[]{:S(2)}, u32[]{:S(2)}) collective-permute-start(f32[4,136,128]{2,1,0:T(8,128)S(1)} %pad_maximum_fusion.8), channel_id=1, source_target_pairs={{0,32},{8,40},{16,48},{24,56},{32,64},{40,72},{48,80},{56,88},{64,... | collective-permute-start | bytes 835592 | tf_op jit(solution)/shard_map/ppermute | solution.py:17
  77.7 10.8 %collective-permute-start.5 = (f32[4,136,128]{2,1,0:T(8,128)S(1)}, f32[4,136,128]{2,1,0:T(8,128)S(1)}, u32[]{:S(2)}, u32[]{:S(2)}) collective-permute-start(f32[4,136,128]{2,1,0:T(8,128)S(1)} %pad_maximum_fusion.9), channel_id=1, source_target_pairs={{0,64},{8,72},{16,80},{24,88},{32,96},{40,104},{48,112},{56,120},{... | collective-permute-start | bytes 835592 | tf_op jit(solution)/shard_map/ppermute | solution.py:17
  84.2 35.0 %copy-start.18 = (pred[512,512]{1,0:T(8,128)(4,1)}, pred[512,512]{1,0:T(8,128)(4,1)S(1)}, u32[]{:S(2)}) copy-start(pred[512,512]{1,0:T(8,128)(4,1)S(1)} %iota_compare_fusion.4) | copy-start | bytes 786436
  88.5 30.0 %collective-permute-start.6 = (f32[4,136,128]{2,1,0:T(8,128)S(1)}, f32[4,136,128]{2,1,0:T(8,128)S(1)}, u32[]{:S(2)}, u32[]{:S(2)}) collective-permute-start(f32[4,136,128]{2,1,0:T(8,128)S(1)} %pad_maximum_fusion.10), channel_id=1, source_target_pairs={{0,128},{8,136},{16,144},{24,152},{32,160},{40,168},{48,176},{56,1... | collective-permute-start | bytes 835592 | tf_op jit(solution)/shard_map/ppermute | solution.py:17
  113.6 5.6 copy-start.7
  118.5 4.3 copy-start.12
  119.2 3.7 copy-start.20
  122.8 70.3 %copy-start.2 = (f32[4,512,128]{1,2,0:T(8,128)}, f32[4,512,128]{1,2,0:T(8,128)S(1)}, u32[]{:S(2)}) copy-start(f32[4,512,128]{1,2,0:T(8,128)S(1)} %get-tuple-element.57) | copy-start | bytes 3145732
  152.4 9.2 %copy-start.24 = (bf16[512,4096]{1,0:T(8,128)(2,1)S(1)}, bf16[512,4096]{1,0:T(8,128)(2,1)}, u32[]{:S(2)}) copy-start(bf16[512,4096]{1,0:T(8,128)(2,1)} %all-gather.6.cloned.1.call-done) | copy-start | bytes 12582916
  158.4 34.7 %copy-start.5 = (bf16[512,512]{0,1:T(8,128)(2,1)}, bf16[512,512]{0,1:T(8,128)(2,1)S(1)}, u32[]{:S(2)}) copy-start(bf16[512,512]{0,1:T(8,128)(2,1)S(1)} %convolution_convert_fusion.4) | copy-start | bytes 1572868
  158.4 3.3 copy-start.11
  160.4 10.9 %collective-permute-start.7 = (f32[4,136,128]{2,1,0:T(8,128)S(1)}, f32[4,136,128]{2,1,0:T(8,128)S(1)}, u32[]{:S(2)}, u32[]{:S(2)}) collective-permute-start(f32[4,136,128]{2,1,0:T(8,128)S(1)} %pad_maximum_fusion.3), channel_id=1, source_target_pairs={{8,0},{16,8},{24,16},{32,24},{40,32},{48,40},{56,48},{64,56},{72,6... | collective-permute-start | bytes 835592 | tf_op jit(solution)/shard_map/ppermute | solution.py:17
  164.1 8.6 %copy-start.8 = (bf16[512,4096]{1,0:T(8,128)(2,1)S(1)}, bf16[512,4096]{1,0:T(8,128)(2,1)}, u32[]{:S(2)}) copy-start(bf16[512,4096]{1,0:T(8,128)(2,1)} %all-gather.8.cloned.1.call-done) | copy-start | bytes 12582916
  171.2 8.5 %copy-start.17 = (f32[4,136,128]{2,1,0:T(8,128)}, f32[4,136,128]{2,1,0:T(8,128)S(1)}, u32[]{:S(2)}) copy-start(f32[4,136,128]{2,1,0:T(8,128)S(1)} %collective-permute-done.7) | copy-start | bytes 835588
  171.2 8.5 %collective-permute-start.8 = (f32[4,136,128]{2,1,0:T(8,128)S(1)}, f32[4,136,128]{2,1,0:T(8,128)}, u32[]{:S(2)}, u32[]{:S(2)}) collective-permute-start(f32[4,136,128]{2,1,0:T(8,128)S(1)} %collective-permute-done.7), channel_id=1, source_target_pairs={{8,0},{16,8},{24,16},{32,24},{40,32},{48,40},{56,48},{64,56},{72,6... | collective-permute-start | bytes 835592 | tf_op jit(solution)/shard_map/ppermute | solution.py:17
  177.2 600.6 %all-gather.10.cloned.1.call-start = ((), (), s32[]{:S(2)}) async-start(), calls=%async_computation.5 | async-start | bytes 69746688 | tf_op jit(solution)/shard_map/all_gather | solution.py:10
  181.6 9.9 %collective-permute-start.9 = (f32[4,136,128]{2,1,0:T(8,128)S(1)}, f32[4,136,128]{2,1,0:T(8,128)S(1)}, u32[]{:S(2)}, u32[]{:S(2)}) collective-permute-start(f32[4,136,128]{2,1,0:T(8,128)S(1)} %pad_maximum_fusion.11), channel_id=1, source_target_pairs={{16,0},{24,8},{32,16},{40,24},{48,32},{56,40},{64,48},{72,56},{80,... | collective-permute-start | bytes 835592 | tf_op jit(solution)/shard_map/ppermute | solution.py:17
  191.6 11.2 %copy-start.16 = (bf16[512,512]{0,1:T(8,128)(2,1)S(1)}, bf16[512,512]{0,1:T(8,128)(2,1)}, u32[]{:S(2)}) copy-start(bf16[512,512]{0,1:T(8,128)(2,1)} %copy-done.15) | copy-start | bytes 1572868
  191.6 11.1 %copy-start.19 = (pred[512,512]{1,0:T(8,128)(4,1)S(1)}, pred[512,512]{1,0:T(8,128)(4,1)}, u32[]{:S(2)}) copy-start(pred[512,512]{1,0:T(8,128)(4,1)} %copy-done.18) | copy-start | bytes 786436
  191.6 9.8 %collective-permute-start.10 = (f32[4,136,128]{2,1,0:T(8,128)S(1)}, f32[4,136,128]{2,1,0:T(8,128)S(1)}, u32[]{:S(2)}, u32[]{:S(2)}) collective-permute-start(f32[4,136,128]{2,1,0:T(8,128)S(1)} %pad_maximum_fusion.12), channel_id=1, source_target_pairs={{32,0},{40,8},{48,16},{56,24},{64,32},{72,40},{80,48},{88,56},{96,... | collective-permute-start | bytes 835592 | tf_op jit(solution)/shard_map/ppermute | solution.py:17
  201.5 14.7 %collective-permute-start.11 = (f32[4,136,128]{2,1,0:T(8,128)S(1)}, f32[4,136,128]{2,1,0:T(8,128)S(1)}, u32[]{:S(2)}, u32[]{:S(2)}) collective-permute-start(f32[4,136,128]{2,1,0:T(8,128)S(1)} %pad_maximum_fusion.13), channel_id=1, source_target_pairs={{64,0},{72,8},{80,16},{88,24},{96,32},{104,40},{112,48},{120,56},{... | collective-permute-start | bytes 835592 | tf_op jit(solution)/shard_map/ppermute | solution.py:17
  202.8 15.0 %copy-start.10 = (bf16[512,512]{0,1:T(8,128)(2,1)S(1)}, bf16[512,512]{0,1:T(8,128)(2,1)}, u32[]{:S(2)}) copy-start(bf16[512,512]{0,1:T(8,128)(2,1)} %copy-done.9) | copy-start | bytes 1572868
  216.3 15.1 %collective-permute-start.12 = (f32[4,136,128]{2,1,0:T(8,128)S(1)}, f32[4,136,128]{2,1,0:T(8,128)S(1)}, u32[]{:S(2)}, u32[]{:S(2)}) collective-permute-start(f32[4,136,128]{2,1,0:T(8,128)S(1)} %pad_maximum_fusion.14), channel_id=1, source_target_pairs={{128,0},{136,8},{144,16},{152,24},{160,32},{168,40},{176,48},{184,... | collective-permute-start | bytes 835592 | tf_op jit(solution)/shard_map/ppermute | solution.py:17
  231.4 1.3 copy-start.3
  231.4 1.4 copy-start.6
  231.4 1.4 copy-start.13
  237.7 3.5 copy-start.14
  237.7 6.5 collective-permute-start.13
  245.4 2.3 copy-start.1
  267.6 16.9 %copy-start.4 = (bf16[3,512,512]{1,2,0:T(8,128)(2,1)S(1)}, bf16[3,512,512]{1,2,0:T(8,128)(2,1)}, u32[]{:S(2)}) copy-start(bf16[3,512,512]{1,2,0:T(8,128)(2,1)} %get-tuple-element.60) | copy-start | bytes 4718596
  267.6 140.8 %all-to-all-start = ((bf16[32,512,128]{2,1,0:T(8,128)(2,1)}), bf16[32,512,128]{2,1,0:T(8,128)(2,1)}, u32[]{:S(2)}, u32[]{:S(2)}) async-start(bf16[32,512,128]{2,1,0:T(8,128)(2,1)} %bitcast.223), calls=%async_computation.1 | async-start | bytes 8388608 | tf_op jit(solution)/shard_map/all_to_all | solution.py:208
Sparse Core Ops, SparseCore 0:
  9.8 36.5 all-gather.5
  48.9 103.5 all-gather.7
  177.3 35.1 reduce-scatter.1
  267.7 510.0 all-gather.9
